TPU v7x, 32 devices: a whole 2x2x4 slice. The times are simulated.
32 devices in a mesh: box: 4 (over x, core), samp: 8 (over z, y).
Axes of the slice: x: 2, y: 2, z: 4, core: 2. Of those that a mesh axis runs over, the one named last changes fastest.
Arguments:
- child_out: float32 [1024, 2, 18432], P(('box', 'samp')), may hold values from -6 to 6
- child_octant: int32 [128, 8], P(('box', 'samp')), may hold values from 0 to 7, each once within a row
- theta_index: int32 [192, 4], replicated, may hold values from 0 to 95, as said below
- theta_weight: float32 [192, 4], replicated, may hold values from -0.2 to 0.6
- phi_index: int32 [384, 4], replicated, may hold values from 0 to 191, as said below
- phi_weight: float32 [384, 4], replicated, may hold values from -0.2 to 0.6
- shift_angle: float32 [8, 192, 384], replicated, may hold values from -3.140625 to 3.140625
- partner_src: int32 [128, 32], replicated, may hold values from 0 to 127
- partner_disp: int32 [128, 32], replicated, may hold values from 0 to 315
- translation: float32 [316, 2, 192, 384], P(None, None, 'samp'), may hold values from -0.75 to 0.75
Outputs:
- child_in: float32 [1024, 2, 18432], P(('box', 'samp'))
Inputs may be any that keep to these rules, and one draw needn't show every extreme that they name: `theta_index`: four stencil indices for each fine theta sample, consecutive coarse samples near it, clipped to the ends so that they may repeat near the poles (repeated weights add). `phi_index`: four consecutive coarse phi samples near each fine phi sample, wrapping around in phi.
All inputs are finite; a program needn't handle non-finite values.
Results may differ from a plain program's by a relative error of at most 0.00007.
Values sent between devices are 32-bit elements; how exact they have to be, the bound alone decides.
A program may use at most 256 MiB of HBM per device.

v0:
```python
import jax
import jax.numpy as jnp
from jax import lax
from jax.sharding import PartitionSpec as P

NT1 = 96
NP1 = 192


PRECISE = lax.Precision.HIGHEST


def stencil(index, weight, count):
    hits = (index[:, :, None] == jnp.arange(count, dtype=jnp.int32)[None, None, :]).astype(
        weight.dtype
    )
    return jnp.sum(weight[:, :, None] * hits, axis=1)


def spread(field, theta_mat, phi_mat):
    wider = jnp.einsum("czap,qp->czaq", field, phi_mat, precision=PRECISE)
    return jnp.einsum("ta,czaq->cztq", theta_mat, wider, precision=PRECISE)


def contract(field, theta_mat, phi_mat):
    narrow = jnp.einsum("ta,cztq->czaq", theta_mat, field, precision=PRECISE)
    return jnp.einsum("czaq,qp->czap", narrow, phi_mat, precision=PRECISE)


def rotate(field, cosine, sine_part):
    real_part = field[:, 0]
    imag_part = field[:, 1]
    return jnp.stack(
        [real_part * cosine - imag_part * sine_part, real_part * sine_part + imag_part * cosine],
        axis=1,
    )


def rotate_back(field, cosine, sine_part):
    real_part = field[:, 0]
    imag_part = field[:, 1]
    return jnp.stack(
        [real_part * cosine + imag_part * sine_part, imag_part * cosine - real_part * sine_part],
        axis=1,
    )


def translate_rows(sources, op_table, src_rows, disp_rows):
    receivers = src_rows.shape[0]
    blocks = 4
    per_block = receivers // blocks

    def block_terms(items):
        src_block, disp_block = items
        picked = jnp.take(sources, src_block, axis=0)
        operators = jnp.take(op_table, disp_block, axis=0)
        real_sum = jnp.sum(
            operators[:, :, 0] * picked[:, :, 0] - operators[:, :, 1] * picked[:, :, 1], axis=1
        )
        imag_sum = jnp.sum(
            operators[:, :, 0] * picked[:, :, 1] + operators[:, :, 1] * picked[:, :, 0], axis=1
        )
        return jnp.stack([real_sum, imag_sum], axis=1)

    result = lax.map(
        block_terms,
        (src_rows.reshape(blocks, per_block, -1), disp_rows.reshape(blocks, per_block, -1)),
    )
    return result.reshape((receivers,) + result.shape[2:])


def local(
    child_out,
    child_octant,
    theta_index,
    theta_weight,
    phi_index,
    phi_weight,
    shift_angle,
    partner_src,
    partner_disp,
    translation,
):
    child_count = child_out.shape[0]
    child_grid = child_out.reshape(child_count, 2, NT1, NP1)
    theta_mat = stencil(theta_index, theta_weight, NT1)
    phi_mat = stencil(phi_index, phi_weight, NP1)
    octants = child_octant.reshape(-1)
    onehot = (octants[:, None] == jnp.arange(8, dtype=jnp.int32)[None, :]).astype(jnp.float32)
    cosine = jnp.einsum("co,otq->ctq", onehot, jnp.cos(shift_angle), precision=PRECISE)
    sine_part = jnp.einsum("co,otq->ctq", onehot, jnp.sin(shift_angle), precision=PRECISE)
    fine_child = rotate(spread(child_grid, theta_mat, phi_mat), cosine, sine_part)
    parents = child_octant.shape[0]
    parent_out = jnp.sum(fine_child.reshape((parents, 8) + fine_child.shape[1:]), axis=1)
    box_rank = lax.axis_index("box")
    group_rows = parents * lax.axis_size("samp")
    theta_local = lax.all_to_all(parent_out, "samp", split_axis=2, concat_axis=0, tiled=True)
    all_sources = lax.all_gather(theta_local, "box", axis=0, tiled=True)
    src_rows = lax.dynamic_slice_in_dim(partner_src, box_rank * group_rows, group_rows, 0)
    disp_rows = lax.dynamic_slice_in_dim(partner_disp, box_rank * group_rows, group_rows, 0)
    incoming = translate_rows(all_sources, translation, src_rows, disp_rows)
    parent_in = lax.all_to_all(incoming, "samp", split_axis=0, concat_axis=2, tiled=True)
    repeated = jnp.broadcast_to(parent_in[:, None], (parents, 8) + parent_in.shape[1:]).reshape(
        (parents * 8,) + parent_in.shape[1:]
    )
    result = contract(rotate_back(repeated, cosine, sine_part), theta_mat, phi_mat)
    return result.reshape(child_count, 2, NT1 * NP1)


def solution(mesh):
    in_specs = (
        P(("box", "samp"), None, None),
        P(("box", "samp"), None),
        P(),
        P(),
        P(),
        P(),
        P(),
        P(),
        P(),
        P(None, None, "samp", None),
    )
    out_specs = P(("box", "samp"), None, None)
    return jax.shard_map(local, mesh=mesh, in_specs=in_specs, out_specs=out_specs, check_vma=False)
```

profile of v0, /device:TPU:1, one launch (start us, length us, event | category | flops | bytes accessed | tf_op | source)
XLA Modules:
  0.0 691.8 jit_solution(15081064876287532546)
XLA Ops:
  42.3 13.1 %fusion.15 = f32[384,32,2,96]{0,3,2,1:T(8,128)S(1)} fusion(f32[32,2,96,192]{3,2,1,0:T(8,128)} %reshape.106, f32[384,192]{0,1:T(8,128)S(1)} %select_reduce_fusion), kind=kOutput, calls=%fused_computation.43 | convolution fusion | flops 5435817984 | bytes 14450688 | tf_op jit(solution)/shard_map/czap,qp->czaq/dot_general | solution.py:21
  56.4 16.3 %fusion.7 = f32[32,2,192,384]{3,2,1,0:T(8,128)S(1)} fusion(f32[384,32,2,96]{0,3,2,1:T(8,128)S(1)} %fusion.15, f32[192,96]{1,0:T(8,128)S(1)} %select_reduce_fusion.1), kind=kOutput, calls=%fused_computation.33 | convolution fusion | flops 5435817984 | bytes 28385280 | tf_op jit(solution)/shard_map/ta,czaq->cztq/dot_general | solution.py:22
  72.7 20.7 %multiply_subtract_fusion = (f32[32,192,384]{2,1,0:T(8,128)}, f32[32,192,384]{2,1,0:T(8,128)}) fusion(f32[32,2,192,384]{3,2,1,0:T(8,128)S(1)} %fusion.7, f32[32,192,384]{2,0,1:T(8,128)} %fusion.10, f32[32,192,384]{2,0,1:T(8,128)} %fusion.12), kind=kLoop, calls=%fused_computation.32 | loop fusion | flops 14155776 | bytes 56623104 | tf_op jit(solution)/shard_map/sub | solution.py:34
  103.0 59.6 %all_to_all.33 = f32[4,2,192,384]{3,1,0,2:T(2,128)S(1)} all-to-all(f32[4,2,192,384]{3,1,0,2:T(2,128)S(1)} %copy.84), channel_id=1, replica_groups=mesh['box'=4,'samp'=8] {'samp'}, dimensions={2} | all-to-all | bytes 4718592 | tf_op jit(solution)/shard_map/all_to_all | solution.py:97
  165.0 64.7 %all-gather.2.cloned.1.call-done = f32[128,2,24,384]{3,2,1,0:T(8,128)} async-done(((f32[32,2,24,384]{3,2,1,0:T(8,128)}), f32[128,2,24,384]{3,2,1,0:T(8,128)}) %all-gather.2.cloned.1.call-update) | async-done | bytes 9437200 | tf_op jit(solution)/shard_map/all_gather | solution.py:98
  229.7 306.9 %while.10 = (s32[]{:T(128)}, f32[4,8,2,24,384]{4,3,2,1,0:T(8,128)S(1)}, s32[4,8,32]{2,1,0:T(8,128)S(1)}, f32[316,2,24,384]{3,2,1,0:T(8,128)}, s32[4,8,32]{2,1,0:...) while((s32[]{:T(128)}, f32[4,8,2,24,384]{4,3,2,1,0:T(8,128)S(1)}, s32[4,8,32]{2,1,0:T(8,128)S(1)}, ...), condition=%wide.region_6.7_spmd, body=%wide.region_3.6_spmd.sunk | while | flops 28318208 | bytes 266034288 | solution.py:65
  229.8 16.8 %gather_fusion = f32[256,2,24,384]{3,2,1,0:T(8,128)} fusion(f32[128,2,24,384]{3,2,1,0:T(8,128)} %get-tuple-element.132, s32[1024]{0:T(1024)S(1)} %pad_clamp_fusion.4), kind=kCustom, calls=%fused_computation.1.clone.1 | custom fusion | bytes 37749760 | tf_op jit(solution)/shard_map/while/body/eval_jaxpr/jit(_take)/gather | solution.py:55
  246.6 12.7 %broadcast_select_fusion.4 = f32[8,32,2,24,384]{4,3,2,1,0:T(8,128)} fusion(f32[8,32,2,24,384]{4,3,2,1,0:T(8,128)} %bitcast.115, pred[8,32]{1,0:T(8,128)(4,1)S(1)} %get-tuple-element.108), kind=kLoop, calls=%fused_computation.4.clone.1 | loop fusion | flops 4718592 | bytes 37748992 | tf_op jit(solution)/shard_map/while/body/eval_jaxpr/jit(_take)/select_n | solution.py:55
  259.3 20.6 %gather_fusion.1 = f32[256,2,24,384]{3,2,1,0:T(8,128)} fusion(f32[316,2,24,384]{3,2,1,0:T(8,128)} %get-tuple-element.130, s32[1024]{0:T(1024)S(1)} %pad_clamp_fusion.5), kind=kCustom, calls=%fused_computation.clone.1 | custom fusion | bytes 37749760 | tf_op jit(solution)/shard_map/while/body/eval_jaxpr/jit(_take)/gather | solution.py:56
  279.9 13.8 %broadcast_select_fusion.5 = f32[8,32,2,24,384]{4,3,2,1,0:T(8,128)} fusion(f32[8,32,2,24,384]{4,3,2,1,0:T(8,128)} %bitcast.116, pred[8,32]{1,0:T(8,128)(4,1)S(1)} %get-tuple-element.110), kind=kLoop, calls=%fused_computation.5.clone.1 | loop fusion | flops 4718592 | bytes 37748992 | tf_op jit(solution)/shard_map/while/body/eval_jaxpr/jit(_take)/select_n | solution.py:56
  306.5 16.8 %gather_fusion = f32[256,2,24,384]{3,2,1,0:T(8,128)} fusion(f32[128,2,24,384]{3,2,1,0:T(8,128)} %get-tuple-element.132, s32[1024]{0:T(1024)S(1)} %pad_clamp_fusion.4), kind=kCustom, calls=%fused_computation.1.clone.1 | custom fusion | bytes 37749760 | tf_op jit(solution)/shard_map/while/body/eval_jaxpr/jit(_take)/gather | solution.py:55
  336.1 20.6 %gather_fusion.1 = f32[256,2,24,384]{3,2,1,0:T(8,128)} fusion(f32[316,2,24,384]{3,2,1,0:T(8,128)} %get-tuple-element.130, s32[1024]{0:T(1024)S(1)} %pad_clamp_fusion.5), kind=kCustom, calls=%fused_computation.clone.1 | custom fusion | bytes 37749760 | tf_op jit(solution)/shard_map/while/body/eval_jaxpr/jit(_take)/gather | solution.py:56
  356.7 13.8 %broadcast_select_fusion.5 = f32[8,32,2,24,384]{4,3,2,1,0:T(8,128)} fusion(f32[8,32,2,24,384]{4,3,2,1,0:T(8,128)} %bitcast.116, pred[8,32]{1,0:T(8,128)(4,1)S(1)} %get-tuple-element.110), kind=kLoop, calls=%fused_computation.5.clone.1 | loop fusion | flops 4718592 | bytes 37748992 | tf_op jit(solution)/shard_map/while/body/eval_jaxpr/jit(_take)/select_n | solution.py:56
  383.3 16.8 %gather_fusion = f32[256,2,24,384]{3,2,1,0:T(8,128)} fusion(f32[128,2,24,384]{3,2,1,0:T(8,128)} %get-tuple-element.132, s32[1024]{0:T(1024)S(1)} %pad_clamp_fusion.4), kind=kCustom, calls=%fused_computation.1.clone.1 | custom fusion | bytes 37749760 | tf_op jit(solution)/shard_map/while/body/eval_jaxpr/jit(_take)/gather | solution.py:55
  400.1 12.7 %broadcast_select_fusion.4 = f32[8,32,2,24,384]{4,3,2,1,0:T(8,128)} fusion(f32[8,32,2,24,384]{4,3,2,1,0:T(8,128)} %bitcast.115, pred[8,32]{1,0:T(8,128)(4,1)S(1)} %get-tuple-element.108), kind=kLoop, calls=%fused_computation.4.clone.1 | loop fusion | flops 4718592 | bytes 37748992 | tf_op jit(solution)/shard_map/while/body/eval_jaxpr/jit(_take)/select_n | solution.py:55
  412.8 20.6 %gather_fusion.1 = f32[256,2,24,384]{3,2,1,0:T(8,128)} fusion(f32[316,2,24,384]{3,2,1,0:T(8,128)} %get-tuple-element.130, s32[1024]{0:T(1024)S(1)} %pad_clamp_fusion.5), kind=kCustom, calls=%fused_computation.clone.1 | custom fusion | bytes 37749760 | tf_op jit(solution)/shard_map/while/body/eval_jaxpr/jit(_take)/gather | solution.py:56
  433.4 13.8 %broadcast_select_fusion.5 = f32[8,32,2,24,384]{4,3,2,1,0:T(8,128)} fusion(f32[8,32,2,24,384]{4,3,2,1,0:T(8,128)} %bitcast.116, pred[8,32]{1,0:T(8,128)(4,1)S(1)} %get-tuple-element.110), kind=kLoop, calls=%fused_computation.5.clone.1 | loop fusion | flops 4718592 | bytes 37748992 | tf_op jit(solution)/shard_map/while/body/eval_jaxpr/jit(_take)/select_n | solution.py:56
  460.0 16.8 %gather_fusion = f32[256,2,24,384]{3,2,1,0:T(8,128)} fusion(f32[128,2,24,384]{3,2,1,0:T(8,128)} %get-tuple-element.132, s32[1024]{0:T(1024)S(1)} %pad_clamp_fusion.4), kind=kCustom, calls=%fused_computation.1.clone.1 | custom fusion | bytes 37749760 | tf_op jit(solution)/shard_map/while/body/eval_jaxpr/jit(_take)/gather | solution.py:55
  489.6 20.6 %gather_fusion.1 = f32[256,2,24,384]{3,2,1,0:T(8,128)} fusion(f32[316,2,24,384]{3,2,1,0:T(8,128)} %get-tuple-element.130, s32[1024]{0:T(1024)S(1)} %pad_clamp_fusion.5), kind=kCustom, calls=%fused_computation.clone.1 | custom fusion | bytes 37749760 | tf_op jit(solution)/shard_map/while/body/eval_jaxpr/jit(_take)/gather | solution.py:56
  510.2 13.8 %broadcast_select_fusion.5 = f32[8,32,2,24,384]{4,3,2,1,0:T(8,128)} fusion(f32[8,32,2,24,384]{4,3,2,1,0:T(8,128)} %bitcast.116, pred[8,32]{1,0:T(8,128)(4,1)S(1)} %get-tuple-element.110), kind=kLoop, calls=%fused_computation.5.clone.1 | loop fusion | flops 4718592 | bytes 37748992 | tf_op jit(solution)/shard_map/while/body/eval_jaxpr/jit(_take)/select_n | solution.py:56
  536.6 58.3 %all_to_all.34 = f32[32,2,24,384]{3,2,1,0:T(8,128)S(1)} all-to-all(f32[32,2,24,384]{3,2,1,0:T(8,128)S(1)} %bitcast.125), channel_id=1, replica_groups=mesh['box'=4,'samp'=8] {'samp'}, dimensions={0} | all-to-all | bytes 4718592 | tf_op jit(solution)/shard_map/all_to_all | solution.py:102
  604.9 21.0 %add_bitcast_fusion = (f32[32,1,192,384]{3,0,2,1:T(8,128)}, f32[32,1,192,384]{3,0,2,1:T(8,128)}) fusion(f32[32,192,384]{2,0,1:T(8,128)} %fusion.10, f32[32,192,384]{2,0,1:T(8,128)} %fusion.12, f32[32,2,192,384]{3,0,2,1:T(8,128)} %broadcast_bitcast_fusion), kind=kLoop, calls=%fused_computation.29 | loop fusion | flops 14155776 | bytes 56623104 | tf_op jit(solution)/shard_map/stack | solution.py:42
  633.0 29.2 %fusion.1 = f32[32,2,384,96]{2,3,1,0:T(8,128)} fusion(f32[32,2,192,384]{3,0,2,1:T(8,128)S(1)} %pad_maximum_fusion, f32[192,96]{1,0:T(8,128)S(1)} %copy-done.4), kind=kOutput, calls=%fused_computation.18 | convolution fusion | flops 5435817984 | bytes 28385280 | tf_op jit(solution)/shard_map/ta,cztq->czaq/dot_general | solution.py:26
  662.2 13.7 %fusion.3 = f32[32,2,96,192]{3,2,1,0:T(8,128)} fusion(f32[32,2,384,96]{2,3,1,0:T(8,128)} %fusion.1, f32[384,192]{0,1:T(8,128)S(1)} %copy-done.2), kind=kOutput, calls=%fused_computation.24 | convolution fusion | flops 5435817984 | bytes 14450688 | tf_op jit(solution)/shard_map/czaq,qp->czap/dot_general | solution.py:27
  (83 shorter events, 151.2 us)
Async XLA Ops:
  6.5 223.2 %all-gather.2.cloned.1.call-start = ((), (), s32[]{:S(2)}) async-start(), calls=%async_computation.2 | async-start | bytes 11796480 | tf_op jit(solution)/shard_map/all_gather | solution.py:98
  27.3 14.8 %copy-start.7 = (f32[384,4]{0,1:T(4,128)S(1)}, f32[384,4]{0,1:T(4,128)}, u32[]{:S(2)}) copy-start(f32[384,4]{0,1:T(4,128)} %param.17) | copy-start | bytes 18436
  27.3 14.8 %copy-start.8 = (s32[384,4]{0,1:T(4,128)S(1)}, s32[384,4]{0,1:T(4,128)}, u32[]{:S(2)}) copy-start(s32[384,4]{0,1:T(4,128)} %param.16) | copy-start | bytes 18436
  42.3 13.1 %copy-start.1 = (f32[384,192]{0,1:T(8,128)}, f32[384,192]{0,1:T(8,128)S(1)}, u32[]{:S(2)}) copy-start(f32[384,192]{0,1:T(8,128)S(1)} %select_reduce_fusion) | copy-start | bytes 884740
  42.3 13.1 %copy-start.9 = (f32[192,4]{0,1:T(4,128)S(1)}, f32[192,4]{0,1:T(4,128)}, u32[]{:S(2)}) copy-start(f32[192,4]{0,1:T(4,128)} %param.15) | copy-start | bytes 9220
  42.3 13.1 %copy-start.10 = (s32[192,4]{0,1:T(4,128)S(1)}, s32[192,4]{0,1:T(4,128)}, u32[]{:S(2)}) copy-start(s32[192,4]{0,1:T(4,128)} %param.14) | copy-start | bytes 9220
  55.7 0.6 copy-start.3
  103.0 61.7 %copy-start.5 = (s32[128,32]{0,1:T(8,128)S(1)}, s32[128,32]{0,1:T(8,128)}, u32[]{:S(2)}) copy-start(s32[128,32]{0,1:T(8,128)} %param.19) | copy-start | bytes 49156
  103.0 61.7 %copy-start.6 = (s32[128,32]{0,1:T(8,128)S(1)}, s32[128,32]{0,1:T(8,128)}, u32[]{:S(2)}) copy-start(s32[128,32]{0,1:T(8,128)} %param.20) | copy-start | bytes 49156
  279.9 18.4 %copy-start = (f32[8,32,2,24,384]{4,3,2,1,0:T(8,128)S(1)}, f32[8,32,2,24,384]{4,3,2,1,0:T(8,128)}, u32[]{:S(2)}) copy-start(f32[8,32,2,24,384]{4,3,2,1,0:T(8,128)} %broadcast_select_fusion.4) | copy-start | bytes 56623108 | tf_op jit(solution)/shard_map/while
  356.7 18.4 %copy-start = (f32[8,32,2,24,384]{4,3,2,1,0:T(8,128)S(1)}, f32[8,32,2,24,384]{4,3,2,1,0:T(8,128)}, u32[]{:S(2)}) copy-start(f32[8,32,2,24,384]{4,3,2,1,0:T(8,128)} %broadcast_select_fusion.4) | copy-start | bytes 56623108 | tf_op jit(solution)/shard_map/while
  433.4 18.4 %copy-start = (f32[8,32,2,24,384]{4,3,2,1,0:T(8,128)S(1)}, f32[8,32,2,24,384]{4,3,2,1,0:T(8,128)}, u32[]{:S(2)}) copy-start(f32[8,32,2,24,384]{4,3,2,1,0:T(8,128)} %broadcast_select_fusion.4) | copy-start | bytes 56623108 | tf_op jit(solution)/shard_map/while
  510.2 18.4 %copy-start = (f32[8,32,2,24,384]{4,3,2,1,0:T(8,128)S(1)}, f32[8,32,2,24,384]{4,3,2,1,0:T(8,128)}, u32[]{:S(2)}) copy-start(f32[8,32,2,24,384]{4,3,2,1,0:T(8,128)} %broadcast_select_fusion.4) | copy-start | bytes 56623108 | tf_op jit(solution)/shard_map/while
  625.8 7.1 %copy-start.4 = (f32[192,96]{1,0:T(8,128)S(1)}, f32[192,96]{1,0:T(8,128)}, u32[]{:S(2)}) copy-start(f32[192,96]{1,0:T(8,128)} %copy-done.3) | copy-start | bytes 221188
  633.0 29.2 %copy-start.2 = (f32[384,192]{0,1:T(8,128)S(1)}, f32[384,192]{0,1:T(8,128)}, u32[]{:S(2)}) copy-start(f32[384,192]{0,1:T(8,128)} %copy-done.1) | copy-start | bytes 884740
Sparse Core Ops, SparseCore 0:
  164.8 64.8 all-gather.1
where the time goes:
time: 703 us; the launch traced here: 692 us
  local copies, waits for them, and re-layouts  213 us (30%)
  other arithmetic  195 us (28%)
  blocking collectives  118 us (17%)
  matrix products  87.3 us (12%)
  waiting for transfers between devices  64.7 us (9%)
  between operations  13.8 us (2%)
    gather x4, local copies, waits for them, and re-layouts, block_terms(): operators = jnp.take(op_table, disp_block, axis=0)  82.4 us
    gather x4, local copies, waits for them, and re-layouts, block_terms(): picked = jnp.take(sources, src_block, axis=0)  67.1 us
    all_gather x1, waiting for transfers between devices, local(): all_sources = lax.all_gather(theta_local, 'box', axis=0, tiled=True)  64.7 us
    all_to_all x1, blocking collectives, local(): lax.all_to_all(parent_out, 'samp', split_axis=2, concat_axis=0, tiled=True)  59.6 us
    all_to_all x1, blocking collectives, local(): lax.all_to_all(incoming, 'samp', split_axis=0, concat_axis=2, tiled=True)  58.3 us
    select_n x4, other arithmetic, block_terms(): operators = jnp.take(op_table, disp_block, axis=0)  55.2 us
    select_n x8, other arithmetic, block_terms(): picked = jnp.take(sources, src_block, axis=0)  50.7 us
    reduce_sum x4, other arithmetic, block_terms(): jnp.sum(operators[:, :, 0] * picked[:, :, 0] - operators[:, :, 1] * picke...  32.2 us
  transfers between devices with their start and end apart: 1, of which 1 were waited for; matrix products, arithmetic and copies ran while one was open for 0% of the time, Pallas kernels for 0%

commit v1 on v0

v1 whole, which is shorter than its diff:
```python
import functools

import jax
import jax.numpy as jnp
from jax import lax
from jax.experimental import pallas as pl
from jax.experimental.pallas import tpu as pltpu
from jax.sharding import PartitionSpec as P

NT1 = 96
NP1 = 192
LANES = 128
MESH = pl.DeviceIdType.MESH
VMEM_LIMIT = 62 * 1024 * 1024


def stencil(index, weight, count):
    hits = (index[:, :, None] == jnp.arange(count, dtype=jnp.int32)[None, None, :]).astype(
        weight.dtype
    )
    return jnp.sum(weight[:, :, None] * hits, axis=1)


def split(values):
    high = values.astype(jnp.bfloat16)
    low = (values - high.astype(jnp.float32)).astype(jnp.bfloat16)
    return high, low


def dot(left, right):
    return jnp.dot(left, right, preferred_element_type=jnp.float32)


def dot3(left, right):
    return dot(left[0], right[0]) + dot(left[1], right[0]) + dot(left[0], right[1])


def aggregate_kernel(
    octant, child, cosine, sine, top_hi, top_lo, low_hi, low_lo, theta, out, wide
):
    parent = pl.program_id(0)
    kids, parts, half, width = child.shape
    field = child[...].reshape(kids * parts * half, width)
    edge = top_hi.shape[0]
    even = split(dot3(split(field[:, :edge]), (top_hi[...], top_lo[...])))
    odd = split(dot3(split(field[:, width - edge :]), (low_hi[...], low_lo[...])))
    for slot, piece in enumerate((even[0], odd[0], even[1], odd[1], even[0], odd[0])):
        wide[:, slot * half : (slot + 1) * half, :] = piece.reshape(kids * parts, half, piece.shape[1])
    out[...] = jnp.zeros_like(out)

    def one_child(kid, carry):
        spot = octant[parent * kids + kid]
        for chunk in range(out.shape[0]):
            lanes = slice(chunk * LANES, (chunk + 1) * LANES)
            real = dot(theta[...], wide[kid * 2, :, lanes])
            imag = dot(theta[...], wide[kid * 2 + 1, :, lanes])
            cos_part = cosine[spot, :, lanes]
            sin_part = sine[spot, :, lanes]
            out[chunk, 0, 0] += real * cos_part - imag * sin_part
            out[chunk, 0, 1] += real * sin_part + imag * cos_part
        return carry

    lax.fori_loop(0, kids, one_child, 0)


def disaggregate_kernel(
    octant, field, cosine, sine, theta_hi, theta_lo, left_hi, left_lo, right_hi, right_lo, out, even_hi, even_lo, odd_hi, odd_lo
):
    parent = pl.program_id(0)
    kids, parts, half, width = out.shape

    def one_child(kid, carry):
        spot = octant[parent * kids + kid]
        for chunk in range(field.shape[0]):
            lanes = slice(chunk * LANES, (chunk + 1) * LANES)
            real = field[chunk, 0, 0]
            imag = field[chunk, 0, 1]
            cos_part = cosine[spot, :, lanes]
            sin_part = sine[spot, :, lanes]
            turned = jnp.concatenate(
                [real * cos_part + imag * sin_part, imag * cos_part - real * sin_part], axis=1
            )
            narrow = split(dot3((theta_hi[...], theta_lo[...]), split(turned)))
            for part in range(parts):
                piece = slice(part * LANES, (part + 1) * LANES)
                even_hi[kid * 2 + part, :, lanes] = narrow[0][:half, piece]
                odd_hi[kid * 2 + part, :, lanes] = narrow[0][half:, piece]
                even_lo[kid * 2 + part, :, lanes] = narrow[1][:half, piece]
                odd_lo[kid * 2 + part, :, lanes] = narrow[1][half:, piece]
        return carry

    lax.fori_loop(0, kids, one_child, 0)

    def flat(ref):
        return ref[...].reshape(kids * parts * half, ref.shape[2])

    left = dot3((flat(even_hi), flat(even_lo)), (left_hi[...], left_lo[...]))
    right = dot3((flat(odd_hi), flat(odd_lo)), (right_hi[...], right_lo[...]))
    edge = left.shape[1]
    shared = 2 * edge - width
    joined = jnp.concatenate(
        [left[:, : edge - shared], left[:, edge - shared :] + right[:, :shared], right[:, shared:]], axis=1
    )
    out[...] = joined.reshape(out.shape)


def exchange_kernel(
    boxes, samps, partners, src_rows, disp_rows, outgoing, table, incoming, *scratch
):
    chunks = outgoing.shape[0]
    sources = scratch[:chunks]
    operators = scratch[chunks : 2 * chunks]
    results = scratch[2 * chunks : 3 * chunks]
    load_sem, own_sem, out_send, out_recv, box_send, box_recv, back_own, back_send, back_recv = scratch[3 * chunks :]
    group = lax.axis_index("box")
    me = lax.axis_index("samp")
    per_device = outgoing.shape[1]
    bits = [1 << i for i in range(boxes.bit_length() - 1)][::-1]

    def mate(bit):
        return group + bit - 2 * bit * lax.rem(lax.div(group, bit), 2)

    barrier = pltpu.get_barrier_semaphore()
    for step in range(1, samps):
        pl.semaphore_signal(barrier, inc=1, device_id=(group, lax.rem(me + step, samps)), device_id_type=MESH)
    for bit in bits:
        pl.semaphore_signal(barrier, inc=1, device_id=(mate(bit), me), device_id_type=MESH)

    def load(chunk):
        return pltpu.make_async_copy(
            table.at[:, :, :, pl.ds(chunk * LANES, LANES)], operators[chunk], load_sem.at[chunk]
        )

    def keep(chunk):
        return pltpu.make_async_copy(
            outgoing.at[chunk, :, :, me], sources[chunk].at[group, me], own_sem.at[chunk]
        )

    def out_copy(chunk, peer, owner):
        return pltpu.make_async_remote_copy(
            src_ref=outgoing.at[chunk, :, :, peer],
            dst_ref=sources[chunk].at[group, owner],
            send_sem=out_send.at[chunk, peer],
            recv_sem=out_recv.at[chunk, owner],
            device_id=(group, peer),
            device_id_type=MESH,
        )

    def back_copy(chunk, peer, owner):
        return pltpu.make_async_remote_copy(
            src_ref=results[chunk].at[peer],
            dst_ref=incoming.at[chunk, :, :, owner],
            send_sem=back_send.at[chunk, peer],
            recv_sem=back_recv.at[chunk, owner],
            device_id=(group, peer),
            device_id_type=MESH,
        )

    def back_keep(chunk):
        return pltpu.make_async_copy(
            results[chunk].at[me], incoming.at[chunk, :, :, me], back_own.at[chunk]
        )

    def box_plan():
        plan = []
        held = [0]
        for bit in bits:
            plan.append((bit, list(held)))
            held = held + [h + bit for h in held]
        return plan

    plan = box_plan()

    def owner_of(mask):
        spot = group
        for bit in bits:
            if mask & bit:
                spot = spot + bit - 2 * bit * lax.rem(lax.div(group, bit), 2)
        return spot

    def hop(chunk, bit, mask):
        return pltpu.make_async_remote_copy(
            src_ref=sources[chunk].at[owner_of(mask)],
            dst_ref=sources[chunk].at[owner_of(mask)],
            send_sem=box_send.at[chunk, mask + bit],
            recv_sem=box_recv.at[chunk, mask + bit],
            device_id=(mate(bit), me),
            device_id_type=MESH,
        )

    def hop_arrival(chunk, mask):
        spot = owner_of(mask)
        return pltpu.make_async_remote_copy(
            src_ref=sources[chunk].at[spot],
            dst_ref=sources[chunk].at[spot],
            send_sem=box_send.at[chunk, mask],
            recv_sem=box_recv.at[chunk, mask],
            device_id=(mate(bits[0]), me),
            device_id_type=MESH,
        )

    for chunk in range(chunks):
        keep(chunk).start()
    for chunk in range(chunks):
        load(chunk).start()
    pl.semaphore_wait(barrier, samps - 1 + len(bits))

    for chunk in range(chunks):

        def send_out(step, carry, chunk=chunk):
            out_copy(chunk, lax.rem(me + step, samps), me).start()
            return carry

        lax.fori_loop(1, samps, send_out, 0)

    def arrive_and_share(chunk):
        def arrived(step, carry):
            peer = lax.rem(me + samps - step, samps)
            out_copy(chunk, peer, peer).wait_recv()
            return carry

        keep(chunk).wait()
        lax.fori_loop(1, samps, arrived, 0)
        for bit, held in plan:
            hop(chunk, bit, 0).start()

    def pass_on(chunk):
        for position, (bit, held) in enumerate(plan):
            for mask in held:
                if mask == 0:
                    continue
                hop(chunk, bit, mask).start()
            if position + 1 < len(plan):
                for mask in [h + bit for h in held]:
                    hop_arrival(chunk, mask).wait_recv()

    def translate(chunk):
        last_bit, last_held = plan[-1]
        for mask in [h + last_bit for h in last_held]:
            hop_arrival(chunk, mask).wait_recv()
        load(chunk).wait()

        def receivers(step, carry):
            peer = lax.rem(me + 1 + step, samps)

            def one(slot, inner):
                row = (peer * per_device + slot) * partners
                real = jnp.zeros(results[chunk].shape[3:], jnp.float32)
                imag = jnp.zeros(results[chunk].shape[3:], jnp.float32)
                for q in range(partners):
                    source = src_rows[row + q]
                    which = disp_rows[row + q]
                    here = lax.div(source, samps * per_device)
                    rest = lax.rem(source, samps * per_device)
                    from_samp = lax.div(rest, per_device)
                    from_slot = lax.rem(rest, per_device)
                    a = sources[chunk][here, from_samp, from_slot, 0]
                    b = sources[chunk][here, from_samp, from_slot, 1]
                    c = operators[chunk][which, 0]
                    d = operators[chunk][which, 1]
                    real = real + (c * a - d * b)
                    imag = imag + (c * b + d * a)
                results[chunk][peer, slot, 0] = real
                results[chunk][peer, slot, 1] = imag
                return inner

            lax.fori_loop(0, per_device, one, 0)

            @pl.when(step > 0)
            def _():
                peer_before = lax.rem(me + step, samps)
                back_copy(chunk, peer_before, me).start()

            return carry

        lax.fori_loop(0, samps, receivers, 0)
        back_keep(chunk).start()

    arrive_and_share(0)
    for chunk in range(chunks):
        if chunk + 1 < chunks:
            arrive_and_share(chunk + 1)
        pass_on(chunk)
        translate(chunk)

    for chunk in range(chunks):

        def finish(step, carry, chunk=chunk):
            there = lax.rem(me + step, samps)
            out_copy(chunk, there, there).wait_send()
            back_copy(chunk, there, there).wait_send()
            back_copy(chunk, there, there).wait_recv()
            return carry

        lax.fori_loop(1, samps, finish, 0)
        for bit, held in plan:
            for mask in held:
                hop(chunk, bit, mask).wait_send()
        back_keep(chunk).wait()


def local(
    boxes,
    samps,
    child_out,
    child_octant,
    theta_index,
    theta_weight,
    phi_index,
    phi_weight,
    shift_angle,
    partner_src,
    partner_disp,
    translation,
):
    child_count, parts, samples = child_out.shape
    parents, kids = child_octant.shape
    rows2, cols2 = shift_angle.shape[1:]
    partners = partner_src.shape[1]
    theta_rows = rows2 // samps
    chunks = cols2 // LANES
    half = NT1 // 2
    width = 2 * NP1
    edge = -(-NP1 // LANES) * LANES
    gap = edge - NP1

    theta_mat = stencil(theta_index, theta_weight, NT1)
    phi_mat = stencil(phi_index, phi_weight, NP1)
    theta_mat = jnp.concatenate([theta_mat[:, 0::2], theta_mat[:, 1::2]], axis=1)

    def parts_of(matrix):
        high = lax.reduce_precision(matrix, 8, 7)
        low = lax.reduce_precision(matrix - high, 8, 7)
        return high.astype(jnp.bfloat16), low.astype(jnp.bfloat16)

    theta_hi, theta_lo = parts_of(theta_mat)
    phi_hi, phi_lo = parts_of(phi_mat)
    theta_all = jnp.concatenate([theta_hi, theta_hi, theta_lo], axis=1)
    before = ((0, 0), (gap, 0))
    after = ((0, 0), (0, gap))
    left = [jnp.pad(m, after) for m in (phi_hi, phi_lo)]
    right = [jnp.pad(m, before) for m in (phi_hi, phi_lo)]
    cosine = jnp.cos(shift_angle)
    sine = jnp.sin(shift_angle)
    octants = child_octant.reshape(-1)
    child = child_out.reshape(child_count, parts, half, width)

    def whole(array):
        return pl.BlockSpec(array.shape, lambda *_: (0,) * array.ndim)

    child_spec = pl.BlockSpec((kids, parts, half, width), lambda i, _: (i, 0, 0, 0))
    parent_spec = pl.BlockSpec((chunks, 1, parts, rows2, LANES), lambda i, _: (0, i, 0, 0, 0))

    extra = [left[0].T, left[1].T, right[0].T, right[1].T, theta_all]
    parent_out = pl.pallas_call(
        aggregate_kernel,
        out_shape=jax.ShapeDtypeStruct((chunks, parents, parts, rows2, LANES), jnp.float32),
        grid_spec=pltpu.PrefetchScalarGridSpec(
            num_scalar_prefetch=1,
            grid=(parents,),
            in_specs=[child_spec, whole(cosine), whole(sine)] + [whole(m) for m in extra],
            out_specs=parent_spec,
            scratch_shapes=[pltpu.VMEM((kids * parts, 3 * NT1, cols2), jnp.bfloat16)],
        ),
        compiler_params=pltpu.CompilerParams(vmem_limit_bytes=VMEM_LIMIT),
    )(octants, child, cosine, sine, *extra)

    group_rows = parents * samps
    start = lax.axis_index("box") * group_rows
    src_rows = lax.dynamic_slice_in_dim(partner_src, start, group_rows, 0).reshape(-1)
    disp_rows = lax.dynamic_slice_in_dim(partner_disp, start, group_rows, 0).reshape(-1)
    block = (parents, parts, theta_rows, LANES)
    anywhere = pl.BlockSpec(memory_space=pl.ANY)
    table = pl.BlockSpec(memory_space=pltpu.SMEM)
    outgoing = parent_out.reshape(chunks, parents, parts, samps, theta_rows, LANES)
    incoming = pl.pallas_call(
        functools.partial(exchange_kernel, boxes, samps, partners),
        out_shape=jax.ShapeDtypeStruct(outgoing.shape, jnp.float32),
        in_specs=[table, table, anywhere, anywhere],
        out_specs=anywhere,
        scratch_shapes=[pltpu.VMEM((boxes, samps) + block, jnp.float32)] * chunks
        + [pltpu.VMEM(translation.shape[:3] + (LANES,), jnp.float32)] * chunks
        + [pltpu.VMEM((samps,) + block, jnp.float32)] * chunks
        + [
            pltpu.SemaphoreType.DMA((chunks,)),
            pltpu.SemaphoreType.DMA((chunks,)),
            pltpu.SemaphoreType.DMA((chunks, samps)),
            pltpu.SemaphoreType.DMA((chunks, samps)),
            pltpu.SemaphoreType.DMA((chunks, boxes)),
            pltpu.SemaphoreType.DMA((chunks, boxes)),
            pltpu.SemaphoreType.DMA((chunks,)),
            pltpu.SemaphoreType.DMA((chunks, samps)),
            pltpu.SemaphoreType.DMA((chunks, samps)),
        ],
        compiler_params=pltpu.CompilerParams(
            collective_id=0, has_side_effects=True, vmem_limit_bytes=VMEM_LIMIT
        ),
    )(src_rows, disp_rows, outgoing, translation)
    parent_in = incoming.reshape(chunks, parents, parts, rows2, LANES)

    extra = [theta_hi.T, theta_lo.T, left[0], left[1], right[0], right[1]]
    child_in = pl.pallas_call(
        disaggregate_kernel,
        out_shape=jax.ShapeDtypeStruct((child_count, parts, half, width), jnp.float32),
        grid_spec=pltpu.PrefetchScalarGridSpec(
            num_scalar_prefetch=1,
            grid=(parents,),
            in_specs=[parent_spec, whole(cosine), whole(sine)] + [whole(m) for m in extra],
            out_specs=child_spec,
            scratch_shapes=[pltpu.VMEM((kids * parts, half, cols2), jnp.bfloat16)] * 4,
        ),
        compiler_params=pltpu.CompilerParams(vmem_limit_bytes=VMEM_LIMIT),
    )(octants, parent_in, cosine, sine, *extra)
    return child_in.reshape(child_count, parts, samples)


def solution(mesh):
    in_specs = (
        P(("box", "samp"), None, None),
        P(("box", "samp"), None),
        P(),
        P(),
        P(),
        P(),
        P(),
        P(),
        P(),
        P(None, None, "samp", None),
    )
    out_specs = P(("box", "samp"), None, None)
    body = functools.partial(local, mesh.shape["box"], mesh.shape["samp"])
    return jax.shard_map(body, mesh=mesh, in_specs=in_specs, out_specs=out_specs, check_vma=False)
```

time: 703 us -> 187 us (0.27); the launches traced: 692 us -> 184 us
  other arithmetic: 195 us -> 1.23 us
  local copies, waits for them, and re-layouts: 213 us -> 33.6 us
  Pallas kernels: 0 us -> 149 us
  blocking collectives: 118 us -> 0 us
  matrix products: 87.3 us -> 0 us
  waiting for transfers between devices: 64.7 us -> 0 us
  between operations: 13.8 us -> 0.13 us
    gather x8 -> x0, local copies, waits for them, and re-layouts: 150 us -> none  [the longest x4 82.4 us: block_terms(): operators = jnp.take(op_table, disp_block, axis=0)]
    pallas_call x0 -> x3, Pallas kernels: none -> 149 us  [the longest x1 106 us: local(): pl.pallas_call(functools.partial(exchange_kernel, boxes, samps, partners)...]
    all_to_all x2 -> x0, blocking collectives: 118 us -> none  [the longest x1 59.6 us: local(): lax.all_to_all(parent_out, 'samp', split_axis=2, concat_axis=0, tiled=True)]
    select_n x12 -> x0, other arithmetic: 106 us -> none  [the longest x4 55.2 us: block_terms(): operators = jnp.take(op_table, disp_block, axis=0)]
    dot_general x6 -> x0, matrix products: 87.3 us -> none  [the longest x1 29.2 us: contract(): narrow = jnp.einsum('ta,cztq->czaq', theta_mat, field, precision=PRECISE)]
    all_gather x1 -> x0, waiting for transfers between devices: 64.7 us -> none  [local(): all_sources = lax.all_gather(theta_local, 'box', axis=0, tiled=True)]
    reduce_sum x5 -> x0, other arithmetic: 40 us -> none  [the longest x4 32.2 us: block_terms(): jnp.sum(operators[:, :, 0] * picked[:, :, 0] - operators[:, :, 1] * picke...]
    another operation x2 -> x0, other arithmetic: 28.1 us -> none  [rotate_back(): jnp.stack([real_part * cosine + imag_part * sine_part, imag_part * cosine...]
  transfers between devices with their start and end apart: 1 -> 0, of which waited for: 1 -> 0; matrix products, arithmetic and copies ran while one was open for 0% -> 0% of each run, Pallas kernels for 0% -> 0%
where the time goes in v1:
time: 187 us; the launch traced here: 184 us
  Pallas kernels  149 us (80%)
  local copies, waits for them, and re-layouts  33.6 us (18%)
    pallas_call x1, Pallas kernels, local(): pl.pallas_call(functools.partial(exchange_kernel, boxes, samps, partners)...  106 us
    pallas_call x1, Pallas kernels, local(): pl.pallas_call(aggregate_kernel, out_shape=jax.ShapeDtypeStruct((chunks,...  22.4 us
    pallas_call x1, Pallas kernels, local(): pl.pallas_call(disaggregate_kernel, out_shape=jax.ShapeDtypeStruct((child...  20.3 us
    sin x1, local copies, waits for them, and re-layouts, local(): sine = jnp.sin(shift_angle)  9.39 us
    reshape x1, local copies, waits for them, and re-layouts, local(): child = child_out.reshape(child_count, parts, half, width)  7.26 us
    reshape x1, local copies, waits for them, and re-layouts, local(): return child_in.reshape(child_count, parts, samples)  6.79 us

profile of v1, /device:TPU:1, one launch (start us, length us, event | category | flops | bytes accessed | tf_op | source)
XLA Modules:
  0.0 184.2 jit_solution(17262768692307048898)
XLA Ops:
  0.0 0.9 select_reduce_fusion
  0.9 0.2 copy.33
  1.1 1.1 fusion.5
  2.2 0.8 copy.37.top_hi
  3.0 0.8 copy.38.top_lo
  3.9 0.8 copy.39.low_hi
  4.7 0.8 copy.40.low_lo
  5.5 0.3 select_reduce_fusion.1
  5.8 1.3 slice.6
  7.0 0.1 copy.42
  7.1 1.3 slice.7
  8.4 0.1 copy.43
  8.6 0.8 copy.41.theta
  9.3 9.4 %fusion.4 = (f32[8,192,384]{2,1,0:T(8,128)}, f32[8,192,384]{2,1,0:T(8,128)}) fusion(f32[8,192,384]{2,1,0:T(8,128)S(1)} %copy-done), kind=kLoop, calls=%fused_computation.20 | loop fusion | bytes 7077888 | tf_op jit(solution)/shard_map/sin | solution.py:344
  18.8 0.6 reshape.25.octant
  19.4 7.3 %reshape.28.child = f32[32,2,48,384]{3,2,1,0:T(8,128)} reshape(f32[32,2,18432]{2,1,0:T(2,128)} %param.10) | data formatting | bytes 9437184 | tf_op jit(solution)/shard_map/reshape | solution.py:346
  26.6 22.4 %shard_map.100 = f32[3,4,2,192,128]{4,3,2,1,0:T(8,128)} custom-call(s32[32]{0:T(128)} %reshape.25.octant, f32[32,2,48,384]{3,2,1,0:T(8,128)} %reshape.28.child, f32[8,192,384]{2,1,0:T(8,128)} %get-tuple-element.6.cosine, f32[8,192,384]{2,1,0:T(8,128)} %get-tuple-element.5.sine, bf16[256,384]{1,0:T(8,128)(2,1)} %copy.37.top_hi, ...), custom_call_target="tpu_custom_call" | custom-call | tf_op jit(solution)/shard_map/pallas_call | solution.py:355
  49.0 0.1 constant_dynamic-slice_fusion
  49.1 0.1 copy.31
  49.1 0.7 reshape.26.src_rows
  49.9 0.7 reshape.27.disp_rows
  50.6 106.5 %shard_map.101 = f32[3,4,2,8,24,128]{5,4,3,2,1,0:T(8,128)} custom-call(s32[1024]{0:T(1024)} %reshape.26.src_rows, s32[1024]{0:T(1024)} %reshape.27.disp_rows, f32[3,4,2,8,24,128]{5,4,3,2,1,0:T(8,128)} %bitcast.14, f32[316,2,24,384]{3,2,1,0:T(8,128)} %table.1), custom_call_target="tpu_custom_call" | custom-call | tf_op jit(solution)/shard_map/pallas_call | solution.py:376
  157.0 20.3 %shard_map.102 = f32[32,2,48,384]{3,2,1,0:T(8,128)} custom-call(s32[32]{0:T(128)} %reshape.25.octant, f32[3,4,2,192,128]{4,3,2,1,0:T(8,128)} %bitcast.15, f32[8,192,384]{2,1,0:T(8,128)} %get-tuple-element.6.cosine, f32[8,192,384]{2,1,0:T(8,128)} %get-tuple-element.5.sine, bf16[96,192]{1,0:T(8,128)(2,1)} %bitcast.16, bf16[96,192]{1,0:T(8,128)(2,1)} %bitcast.17, ...), custom_call_target="tpu_custom_call" | custom-call | tf_op jit(solution)/shard_map/pallas_call | solution.py:402
  177.4 6.8 %reshape.31 = f32[32,2,18432]{2,1,0:T(2,128)} reshape(f32[32,2,48,384]{3,2,1,0:T(8,128)} %shard_map.102) | data formatting | bytes 9437184 | tf_op jit(solution)/shard_map/reshape | solution.py:414
  (20 shorter events, 0.2 us)
Async XLA Ops:
  0.9 4.6 %copy-start.5 = (f32[192,4]{0,1:T(4,128)S(1)}, f32[192,4]{0,1:T(4,128)}, u32[]{:S(2)}) copy-start(f32[192,4]{0,1:T(4,128)} %param.13) | copy-start | bytes 9220
  0.9 4.6 %copy-start.6 = (s32[192,4]{0,1:T(4,128)S(1)}, s32[192,4]{0,1:T(4,128)}, u32[]{:S(2)}) copy-start(s32[192,4]{0,1:T(4,128)} %param.12) | copy-start | bytes 9220
  1.1 8.2 %copy-start = (f32[8,192,384]{2,1,0:T(8,128)S(1)}, f32[8,192,384]{2,1,0:T(8,128)}, u32[]{:S(2)}) copy-start(f32[8,192,384]{2,1,0:T(8,128)} %param.16) | copy-start | bytes 7077892
  8.5 10.2 %copy-start.1 = (bf16[192,96]{0,1:T(8,128)(2,1)}, bf16[192,96]{0,1:T(8,128)(2,1)S(1)}, u32[]{:S(2)}) copy-start(bf16[192,96]{0,1:T(8,128)(2,1)S(1)} %get-tuple-element.17) | copy-start | bytes 110596
  8.5 10.2 %copy-start.2 = (bf16[192,96]{0,1:T(8,128)(2,1)}, bf16[192,96]{0,1:T(8,128)(2,1)S(1)}, u32[]{:S(2)}) copy-start(bf16[192,96]{0,1:T(8,128)(2,1)S(1)} %get-tuple-element.18) | copy-start | bytes 110596
  9.3 9.4 %copy-start.7 = (s32[4,8]{1,0:T(4,128)S(1)}, s32[4,8]{1,0:T(4,128)}, u32[]{:S(2)}) copy-start(s32[4,8]{1,0:T(4,128)} %param.11) | copy-start | bytes 388
  26.6 22.4 %copy-start.3 = (s32[128,32]{0,1:T(8,128)S(1)}, s32[128,32]{0,1:T(8,128)}, u32[]{:S(2)}) copy-start(s32[128,32]{0,1:T(8,128)} %param.18) | copy-start | bytes 49156
  26.6 22.4 %copy-start.4 = (s32[128,32]{0,1:T(8,128)S(1)}, s32[128,32]{0,1:T(8,128)}, u32[]{:S(2)}) copy-start(s32[128,32]{0,1:T(8,128)} %param.17) | copy-start | bytes 49156

commit v2 on v1

v2 whole, which is shorter than its diff:
```python
import functools

import jax
import jax.numpy as jnp
from jax import lax
from jax.experimental import pallas as pl
from jax.experimental.pallas import tpu as pltpu
from jax.sharding import PartitionSpec as P

NT1 = 96
NP1 = 192
LANES = 128
MESH = pl.DeviceIdType.MESH
VMEM_LIMIT = 62 * 1024 * 1024


def split(values):
    high = values.astype(jnp.bfloat16)
    low = (values - high.astype(jnp.float32)).astype(jnp.bfloat16)
    return high, low


def dot(left, right):
    return jnp.dot(left, right, preferred_element_type=jnp.float32)


def stencil(wanted, index, weight, axis):
    total = jnp.zeros(wanted.shape, jnp.float32)
    for j in range(index.shape[axis]):
        one = slice(j, j + 1)
        spot = (slice(None), one) if axis == 1 else (one, slice(None))
        total = total + jnp.where(wanted == index[spot], weight[spot], 0.0)
    return total


def iota(shape, axis):
    return lax.broadcasted_iota(jnp.int32, shape, axis)


HALF_PI = (1.5703125, 4.837512969970703e-4, 7.54978995489188e-8)


def cos_sin(angle):
    turns = jnp.floor(angle * 0.6366197723675814 + 0.5)
    rest = ((angle - turns * HALF_PI[0]) - turns * HALF_PI[1]) - turns * HALF_PI[2]
    square = rest * rest
    sine = -1.9515295891e-4 * square + 8.3321608736e-3
    sine = (sine * square - 1.6666654611e-1) * square * rest + rest
    cosine = 2.443315711809948e-5 * square - 1.388731625493765e-3
    cosine = (cosine * square + 4.166664568298827e-2) * square * square - 0.5 * square + 1.0
    half = jnp.floor(turns * 0.5)
    odd = turns - 2.0 * half > 0.5
    flip = half - 2.0 * jnp.floor(half * 0.5) > 0.5
    sin_part = jnp.where(odd, cosine, sine)
    cos_part = jnp.where(odd, -sine, cosine)
    return jnp.where(flip, -cos_part, cos_part), jnp.where(flip, -sin_part, sin_part)


def step_kernel(
    boxes,
    samps,
    partners,
    src_rows,
    disp_rows,
    octant,
    theta_index,
    theta_weight,
    theta_index_t,
    theta_weight_t,
    phi_index,
    phi_weight,
    phi_index_t,
    phi_weight_t,
    child,
    angle,
    table,
    result,
    field,
    wide,
    wide_out,
    grid_sum,
    theta_up,
    theta_down,
    *scratch,
):
    count, parts, half, width = child.shape
    chunks = angle.shape[2] // LANES
    rows2 = angle.shape[1]
    sources = scratch[:chunks]
    operators = scratch[chunks : 2 * chunks]
    results = scratch[2 * chunks : 3 * chunks]
    outgoing = scratch[3 * chunks : 4 * chunks]
    incoming = scratch[4 * chunks : 5 * chunks]
    cosines = scratch[5 * chunks : 6 * chunks]
    sines = scratch[6 * chunks : 7 * chunks]
    (
        child_sem,
        angle_sem,
        result_sem,
        load_sem,
        own_sem,
        out_send,
        out_recv,
        box_send,
        box_recv,
        back_own,
        back_send,
        back_recv,
    ) = scratch[7 * chunks :]
    per_device = outgoing[0].shape[0]
    kids = count // per_device
    theta_rows = rows2 // samps
    edge = -(-(width // 2) // LANES) * LANES
    gap = edge - width // 2
    group = lax.axis_index("box")
    me = lax.axis_index("samp")
    bits = [1 << i for i in range(boxes.bit_length() - 1)][::-1]

    def mate(bit):
        return group + bit - 2 * bit * lax.rem(lax.div(group, bit), 2)

    barrier = pltpu.get_barrier_semaphore()
    for step in range(1, samps):
        pl.semaphore_signal(barrier, inc=1, device_id=(group, lax.rem(me + step, samps)), device_id_type=MESH)
    for bit in bits:
        pl.semaphore_signal(barrier, inc=1, device_id=(mate(bit), me), device_id_type=MESH)

    def load(chunk):
        return pltpu.make_async_copy(
            table.at[:, :, :, pl.ds(chunk * LANES, LANES)], operators[chunk], load_sem.at[chunk]
        )

    def keep(chunk):
        return pltpu.make_async_copy(
            outgoing[chunk].at[:, :, me], sources[chunk].at[group, me], own_sem.at[chunk]
        )

    def out_copy(chunk, peer, owner):
        return pltpu.make_async_remote_copy(
            src_ref=outgoing[chunk].at[:, :, peer],
            dst_ref=sources[chunk].at[group, owner],
            send_sem=out_send.at[chunk, peer],
            recv_sem=out_recv.at[chunk, owner],
            device_id=(group, peer),
            device_id_type=MESH,
        )

    def back_copy(chunk, peer, owner):
        return pltpu.make_async_remote_copy(
            src_ref=results[chunk].at[peer],
            dst_ref=incoming[chunk].at[:, :, owner],
            send_sem=back_send.at[chunk, peer],
            recv_sem=back_recv.at[chunk, owner],
            device_id=(group, peer),
            device_id_type=MESH,
        )

    def back_keep(chunk):
        return pltpu.make_async_copy(
            results[chunk].at[me], incoming[chunk].at[:, :, me], back_own.at[chunk]
        )

    def box_plan():
        plan = []
        held = [0]
        for bit in bits:
            plan.append((bit, list(held)))
            held = held + [h + bit for h in held]
        return plan

    plan = box_plan()

    def owner_of(mask):
        spot = group
        for bit in bits:
            if mask & bit:
                spot = spot + bit - 2 * bit * lax.rem(lax.div(group, bit), 2)
        return spot

    def hop(chunk, bit, mask):
        return pltpu.make_async_remote_copy(
            src_ref=sources[chunk].at[owner_of(mask)],
            dst_ref=sources[chunk].at[owner_of(mask)],
            send_sem=box_send.at[chunk, mask + bit],
            recv_sem=box_recv.at[chunk, mask + bit],
            device_id=(mate(bit), me),
            device_id_type=MESH,
        )

    def hop_arrival(chunk, mask):
        spot = owner_of(mask)
        return pltpu.make_async_remote_copy(
            src_ref=sources[chunk].at[spot],
            dst_ref=sources[chunk].at[spot],
            send_sem=box_send.at[chunk, mask],
            recv_sem=box_recv.at[chunk, mask],
            device_id=(mate(bits[0]), me),
            device_id_type=MESH,
        )

    def load_angle(chunk):
        return pltpu.make_async_copy(
            angle.at[:, :, pl.ds(chunk * LANES, LANES)], cosines[chunk], angle_sem.at[chunk]
        )

    load_child = pltpu.make_async_copy(child, field, child_sem)

    def give(parent):
        rows = pl.ds(parent * kids, kids)
        return pltpu.make_async_copy(field.at[rows], result.at[rows], result_sem.at[parent])

    def build_theta():
        column = iota(theta_up.shape, 1)
        spot = lax.rem(column, 2 * half)
        sample = jnp.where(spot < half, 2 * spot, 2 * (spot - half) + 1)
        high, low = split(stencil(sample, theta_index, theta_weight, 1))
        theta_up[...] = jnp.where(column < 4 * half, high.astype(jnp.float32), low.astype(jnp.float32)).astype(
            jnp.bfloat16
        )
        spot = iota((2 * half, rows2), 0)
        sample = jnp.where(spot < half, 2 * spot, 2 * (spot - half) + 1)
        high, low = split(stencil(sample, theta_index_t, theta_weight_t, 0))
        theta_down[: 2 * half] = high
        theta_down[2 * half :] = low

    def turn(chunk):
        def one(spot, carry):
            cos_part, sin_part = cos_sin(cosines[chunk][spot])
            cosines[chunk][spot] = cos_part
            sines[chunk][spot] = sin_part
            return carry

        lax.fori_loop(0, cosines[chunk].shape[0], one, 0)

    def aggregate(chunk):
        lanes = slice(chunk * LANES, (chunk + 1) * LANES)
        sample = iota((edge, LANES), 0)
        mats = []
        for shift in (0, gap):
            high, low = split(stencil(sample - shift, phi_index_t[:, lanes], phi_weight_t[:, lanes], 0))
            mats.append(jnp.concatenate([high, low], axis=1))

        def one_parent(parent, carry):
            block = field[pl.ds(parent * kids, kids)].reshape(kids * parts * half, width)
            pieces = []
            for mat, start in zip(mats, (0, width - edge)):
                high, low = split(block[:, start : start + edge])
                both = dot(high, mat)
                pieces.append(split(both[:, :LANES] + (both[:, LANES:] + dot(low, mat[:, :LANES]))))
            even, odd = pieces
            for slot, piece in enumerate((even[0], odd[0], even[1], odd[1], even[0], odd[0])):
                piece = piece.reshape(kids, parts, half, LANES)
                for part in range(parts):
                    wide[:, slot * half : (slot + 1) * half, part * LANES : (part + 1) * LANES] = piece[:, part]
            grid_sum[...] = jnp.zeros_like(grid_sum)

            def one_child(kid, inner):
                spot = octant[parent * kids + kid]
                fine = dot(theta_up[...], wide[kid])
                real, imag = fine[:, :LANES], fine[:, LANES:]
                cos_part = cosines[chunk][spot]
                sin_part = sines[chunk][spot]
                grid_sum[0] += real * cos_part - imag * sin_part
                grid_sum[1] += real * sin_part + imag * cos_part
                return inner

            lax.fori_loop(0, kids, one_child, 0)
            for part in range(parts):
                for owner in range(samps):
                    outgoing[chunk][parent, part, owner] = grid_sum[
                        part, owner * theta_rows : (owner + 1) * theta_rows
                    ]
            return carry

        lax.fori_loop(0, per_device, one_parent, 0)

    def disaggregate(chunk, first, last):
        rows = slice(chunk * LANES, (chunk + 1) * LANES)
        sample = iota((LANES, edge), 1)
        mats = []
        for shift in (0, gap):
            high, low = split(stencil(sample - shift, phi_index[rows], phi_weight[rows], 1))
            mats.append((jnp.concatenate([high, high], axis=0), low))

        def one_parent(parent, carry):
            for part in range(parts):
                for owner in range(samps):
                    grid_sum[part, owner * theta_rows : (owner + 1) * theta_rows] = incoming[chunk][
                        parent, part, owner
                    ]

            def one_child(kid, inner):
                spot = octant[parent * kids + kid]
                real, imag = grid_sum[0], grid_sum[1]
                cos_part = cosines[chunk][spot]
                sin_part = sines[chunk][spot]
                turned = jnp.concatenate(
                    [real * cos_part + imag * sin_part, imag * cos_part - real * sin_part], axis=1
                )
                high, low = split(turned)
                both = dot(theta_down[...], high)
                narrow = both[: 2 * half] + (both[2 * half :] + dot(theta_down[: 2 * half], low))
                for place, piece in enumerate(split(narrow)):
                    for parity in range(2):
                        for part in range(parts):
                            wide_out[
                                parity, kid * parts + part, :, place * LANES : (place + 1) * LANES
                            ] = piece[parity * half : (parity + 1) * half, part * LANES : (part + 1) * LANES]
                return inner

            lax.fori_loop(0, kids, one_child, 0)
            ends = []
            for parity in range(2):
                flat = wide_out[parity].reshape(kids * parts * half, 2 * LANES)
                ends.append(dot(flat, mats[parity][0]) + dot(flat[:, :LANES], mats[parity][1]))
            left, right = ends
            shared = 2 * edge - width
            joined = jnp.concatenate(
                [left[:, : edge - shared], left[:, edge - shared :] + right[:, :shared], right[:, shared:]],
                axis=1,
            ).reshape(kids, parts, half, width)
            spot = pl.ds(parent * kids, kids)
            if first:
                field[spot] = joined
            else:
                field[spot] += joined
            if last:

                @pl.when(parent > 0)
                def _():
                    give(parent - 1).start()

            return carry

        lax.fori_loop(0, per_device, one_parent, 0)

    def send_out(chunk):
        def one(step, carry):
            out_copy(chunk, lax.rem(me + step, samps), me).start()
            return carry

        lax.fori_loop(1, samps, one, 0)
        keep(chunk).start()

    load_child.start()
    for chunk in range(chunks):
        load_angle(chunk).start()
    for chunk in range(chunks):
        load(chunk).start()
    build_theta()
    load_angle(0).wait()
    turn(0)
    load_child.wait()
    aggregate(0)
    for chunk in range(1, chunks):
        load_angle(chunk).wait()
        turn(chunk)
        if chunk == 1:
            pl.semaphore_wait(barrier, samps - 1 + len(bits))
        send_out(chunk - 1)
        aggregate(chunk)

    def arrive_and_share(chunk):
        def arrived(step, carry):
            peer = lax.rem(me + samps - step, samps)
            out_copy(chunk, peer, peer).wait_recv()
            return carry

        keep(chunk).wait()
        lax.fori_loop(1, samps, arrived, 0)
        for bit, held in plan:
            hop(chunk, bit, 0).start()

    def pass_on(chunk):
        for position, (bit, held) in enumerate(plan):
            for mask in held:
                if mask == 0:
                    continue
                hop(chunk, bit, mask).start()
            if position + 1 < len(plan):
                for mask in [h + bit for h in held]:
                    hop_arrival(chunk, mask).wait_recv()

    def translate(chunk):
        last_bit, last_held = plan[-1]
        for mask in [h + last_bit for h in last_held]:
            hop_arrival(chunk, mask).wait_recv()
        load(chunk).wait()

        def receivers(step, carry):
            peer = lax.rem(me + 1 + step, samps)

            def one(slot, inner):
                row = (peer * per_device + slot) * partners
                real = jnp.zeros(results[chunk].shape[3:], jnp.float32)
                imag = jnp.zeros(results[chunk].shape[3:], jnp.float32)
                for q in range(partners):
                    source = src_rows[row + q]
                    which = disp_rows[row + q]
                    here = lax.div(source, samps * per_device)
                    rest = lax.rem(source, samps * per_device)
                    from_samp = lax.div(rest, per_device)
                    from_slot = lax.rem(rest, per_device)
                    a = sources[chunk][here, from_samp, from_slot, 0]
                    b = sources[chunk][here, from_samp, from_slot, 1]
                    c = operators[chunk][which, 0]
                    d = operators[chunk][which, 1]
                    real = real + (c * a - d * b)
                    imag = imag + (c * b + d * a)
                results[chunk][peer, slot, 0] = real
                results[chunk][peer, slot, 1] = imag
                return inner

            lax.fori_loop(0, per_device, one, 0)

            @pl.when(step > 0)
            def _():
                peer_before = lax.rem(me + step, samps)
                back_copy(chunk, peer_before, me).start()

            return carry

        lax.fori_loop(0, samps, receivers, 0)

    def returned(chunk):
        def one(step, carry):
            there = lax.rem(me + samps - step, samps)
            back_copy(chunk, there, there).wait_recv()
            return carry

        lax.fori_loop(1, samps, one, 0)
        back_keep(chunk).wait()

    arrive_and_share(0)
    send_out(chunks - 1)
    for chunk in range(chunks):
        if chunk + 1 < chunks:
            arrive_and_share(chunk + 1)
        pass_on(chunk)
        if chunk:
            back_keep(chunk - 1).start()
        translate(chunk)
    for chunk in range(chunks):
        if chunk == chunks - 1 and chunks == 1:
            back_keep(chunk).start()
        returned(chunk)
        disaggregate(chunk, chunk == 0, chunk == chunks - 1)
        if chunk == 0 and chunks > 1:
            back_keep(chunks - 1).start()
    give(per_device - 1).start()

    for chunk in range(chunks):

        def finish(step, carry, chunk=chunk):
            there = lax.rem(me + step, samps)
            out_copy(chunk, there, there).wait_send()
            back_copy(chunk, there, there).wait_send()
            return carry

        lax.fori_loop(1, samps, finish, 0)
        for bit, held in plan:
            for mask in held:
                hop(chunk, bit, mask).wait_send()
    for parent in range(per_device):
        give(parent).wait()


def local(
    boxes,
    samps,
    child_out,
    child_octant,
    theta_index,
    theta_weight,
    phi_index,
    phi_weight,
    shift_angle,
    partner_src,
    partner_disp,
    translation,
):
    child_count, parts, samples = child_out.shape
    parents, kids = child_octant.shape
    octant_count, rows2, cols2 = shift_angle.shape
    partners = partner_src.shape[1]
    theta_rows = rows2 // samps
    chunks = cols2 // LANES
    half = NT1 // 2
    width = 2 * NP1
    child = child_out.reshape(child_count, parts, half, width)
    group_rows = parents * samps
    start = lax.axis_index("box") * group_rows
    src_rows = lax.dynamic_slice_in_dim(partner_src, start, group_rows, 0).reshape(-1)
    disp_rows = lax.dynamic_slice_in_dim(partner_disp, start, group_rows, 0).reshape(-1)
    block = (parents, parts, theta_rows, LANES)
    spread = (parents, parts, samps, theta_rows, LANES)
    turns = (octant_count, rows2, LANES)
    anywhere = pl.BlockSpec(memory_space=pl.ANY)
    scalars = pl.BlockSpec(memory_space=pltpu.SMEM)
    vectors = pl.BlockSpec(memory_space=pltpu.VMEM)
    dma = pltpu.SemaphoreType.DMA

    def per_chunk(shape):
        return [pltpu.VMEM(shape, jnp.float32)] * chunks

    child_in = pl.pallas_call(
        functools.partial(step_kernel, boxes, samps, partners),
        out_shape=jax.ShapeDtypeStruct(child.shape, jnp.float32),
        in_specs=[scalars] * 3 + [vectors] * 8 + [anywhere] * 3,
        out_specs=anywhere,
        scratch_shapes=[
            pltpu.VMEM(child.shape, jnp.float32),
            pltpu.VMEM((kids, 3 * NT1, parts * LANES), jnp.bfloat16),
            pltpu.VMEM((2, kids * parts, half, 2 * LANES), jnp.bfloat16),
            pltpu.VMEM((parts, rows2, LANES), jnp.float32),
            pltpu.VMEM((rows2, 3 * NT1), jnp.bfloat16),
            pltpu.VMEM((2 * NT1, rows2), jnp.bfloat16),
        ]
        + per_chunk((boxes, samps) + block)
        + per_chunk(translation.shape[:3] + (LANES,))
        + per_chunk((samps,) + block)
        + per_chunk(spread)
        + per_chunk(spread)
        + per_chunk(turns)
        + per_chunk(turns)
        + [
            dma(()),
            dma((chunks,)),
            dma((parents,)),
            dma((chunks,)),
            dma((chunks,)),
            dma((chunks, samps)),
            dma((chunks, samps)),
            dma((chunks, boxes)),
            dma((chunks, boxes)),
            dma((chunks,)),
            dma((chunks, samps)),
            dma((chunks, samps)),
        ],
        compiler_params=pltpu.CompilerParams(
            collective_id=0, has_side_effects=True, vmem_limit_bytes=VMEM_LIMIT
        ),
    )(
        src_rows,
        disp_rows,
        child_octant.reshape(-1),
        theta_index,
        theta_weight,
        theta_index.T,
        theta_weight.T,
        phi_index,
        phi_weight,
        phi_index.T,
        phi_weight.T,
        child,
        shift_angle,
        translation,
    )
    return child_in.reshape(child_count, parts, samples)


def solution(mesh):
    in_specs = (
        P(("box", "samp"), None, None),
        P(("box", "samp"), None),
        P(),
        P(),
        P(),
        P(),
        P(),
        P(),
        P(),
        P(None, None, "samp", None),
    )
    out_specs = P(("box", "samp"), None, None)
    body = functools.partial(local, mesh.shape["box"], mesh.shape["samp"])
    return jax.shard_map(body, mesh=mesh, in_specs=in_specs, out_specs=out_specs, check_vma=False)
```

time: 187 us -> 167 us (0.89)
  the two profiles are of different devices: /device:TPU:1 before, /device:TPU:13 now
where the time goes in v2:
time: 167 us; the launch traced here: 166 us
  Pallas kernels  143 us (86%)
  local copies, waits for them, and re-layouts  23.7 us (14%)
    pallas_call x1, Pallas kernels, local(): pl.pallas_call(functools.partial(step_kernel, boxes, samps, partners), ou...  143 us
    reshape x1, local copies, waits for them, and re-layouts, local(): child = child_out.reshape(child_count, parts, half, width)  7.26 us
    reshape x1, local copies, waits for them, and re-layouts, local(): return child_in.reshape(child_count, parts, samples)  6.8 us
    unnamed x4, local copies, waits for them, and re-layouts  5.96 us

profile of v2, /device:TPU:13, one launch (start us, length us, event | category | flops | bytes accessed | tf_op | source)
XLA Modules:
  0.0 166.3 jit_solution(12393459321770624397)
XLA Ops:
  0.0 1.4 reshape.17.octant
  1.4 0.8 constant_dynamic-slice_fusion
  2.2 0.1 copy.16
  2.2 0.7 reshape.16.disp_rows
  2.9 0.1 copy.15
  3.0 0.7 reshape.15.src_rows
  3.6 1.4 copy.17.theta_index
  5.1 1.5 copy.18.theta_weight
  6.6 1.5 copy.19.phi_index
  8.1 1.5 copy.20.phi_weight
  9.6 7.3 %reshape.18.child = f32[32,2,48,384]{3,2,1,0:T(8,128)} reshape(f32[32,2,18432]{2,1,0:T(2,128)} %param.10) | data formatting | bytes 9437184 | tf_op jit(solution)/shard_map/reshape | solution.py:490
  16.9 142.6 %shard_map.100 = f32[32,2,48,384]{3,2,1,0:T(8,128)} custom-call(s32[1024]{0:T(1024)} %reshape.15.src_rows, s32[1024]{0:T(1024)} %reshape.16.disp_rows, s32[32]{0:T(128)} %reshape.17.octant, s32[192,4]{1,0:T(8,128)} %copy.17.theta_index, f32[192,4]{1,0:T(8,128)} %copy.18.theta_weight, s32[4,192]{1,0:T(4,128)} %bitcast.8, f32[4,192]{1,0:T(4,128)} %bitcast.9, ...), custom_call_target="tpu_custom_call" | custom-call | tf_op jit(solution)/shard_map/pallas_call | solution.py:506
  159.5 6.8 %reshape.19 = f32[32,2,18432]{2,1,0:T(2,128)} reshape(f32[32,2,48,384]{3,2,1,0:T(8,128)} %shard_map.100) | data formatting | bytes 9437184 | tf_op jit(solution)/shard_map/reshape | solution.py:559

commit v3 on v2

--- a/solution.py
+++ b/solution.py
@@ -63,12 +63,8 @@
     src_rows,
     disp_rows,
     octant,
-    theta_index,
-    theta_weight,
     theta_index_t,
     theta_weight_t,
-    phi_index,
-    phi_weight,
     phi_index_t,
     phi_weight_t,
     child,
@@ -135,12 +131,35 @@
             outgoing[chunk].at[:, :, me], sources[chunk].at[group, me], own_sem.at[chunk]
         )
 
+    def out_part(chunk, parent, peer):
+        return pltpu.make_async_remote_copy(
+            src_ref=outgoing[chunk].at[parent, :, peer],
+            dst_ref=sources[chunk].at[group, me, parent],
+            send_sem=out_send.at[chunk, peer],
+            recv_sem=out_recv.at[chunk, me],
+            device_id=(group, peer),
+            device_id_type=MESH,
+        )
+
     def out_copy(chunk, peer, owner):
         return pltpu.make_async_remote_copy(
             src_ref=outgoing[chunk].at[:, :, peer],
             dst_ref=sources[chunk].at[group, owner],
             send_sem=out_send.at[chunk, peer],
             recv_sem=out_recv.at[chunk, owner],
+            device_id=(group, peer),
+            device_id_type=MESH,
+        )
+
+    def back_slot(chunk, slot):
+        return chunk + (slot if chunk == chunks - 1 else 0)
+
+    def back_part(chunk, slot, peer, owner):
+        return pltpu.make_async_remote_copy(
+            src_ref=results[chunk].at[peer, slot],
+            dst_ref=incoming[chunk].at[slot, :, owner],
+            send_sem=back_send.at[chunk, peer],
+            recv_sem=back_recv.at[back_slot(chunk, slot), owner],
             device_id=(group, peer),
             device_id_type=MESH,
         )
@@ -210,16 +229,14 @@
         return pltpu.make_async_copy(field.at[rows], result.at[rows], result_sem.at[parent])
 
     def build_theta():
-        column = iota(theta_up.shape, 1)
-        spot = lax.rem(column, 2 * half)
-        sample = jnp.where(spot < half, 2 * spot, 2 * (spot - half) + 1)
-        high, low = split(stencil(sample, theta_index, theta_weight, 1))
-        theta_up[...] = jnp.where(column < 4 * half, high.astype(jnp.float32), low.astype(jnp.float32)).astype(
-            jnp.bfloat16
-        )
         spot = iota((2 * half, rows2), 0)
         sample = jnp.where(spot < half, 2 * spot, 2 * (spot - half) + 1)
-        high, low = split(stencil(sample, theta_index_t, theta_weight_t, 0))
+        narrow = stencil(sample, theta_index_t, theta_weight_t, 0)
+        high, low = split(narrow.T)
+        theta_up[:, : 2 * half] = high
+        theta_up[:, 2 * half : 4 * half] = high
+        theta_up[:, 4 * half :] = low
+        high, low = split(narrow)
         theta_down[: 2 * half] = high
         theta_down[2 * half :] = low
 
@@ -231,6 +248,17 @@
             return carry
 
         lax.fori_loop(0, cosines[chunk].shape[0], one, 0)
+
+    def send_out(chunk, parent):
+        def one(step, carry):
+            out_part(chunk, parent, lax.rem(me + step, samps)).start()
+            return carry
+
+        lax.fori_loop(1, samps, one, 0)
+
+    def send_last(chunk):
+        send_out(chunk, per_device - 1)
+        keep(chunk).start()
 
     def aggregate(chunk):
         lanes = slice(chunk * LANES, (chunk + 1) * LANES)
@@ -255,7 +283,7 @@
             grid_sum[...] = jnp.zeros_like(grid_sum)
 
             def one_child(kid, inner):
-                spot = octant[parent * kids + kid]
+                spot = octant[parent, kid]
                 fine = dot(theta_up[...], wide[kid])
                 real, imag = fine[:, :LANES], fine[:, LANES:]
                 cos_part = cosines[chunk][spot]
@@ -270,19 +298,26 @@
                     outgoing[chunk][parent, part, owner] = grid_sum[
                         part, owner * theta_rows : (owner + 1) * theta_rows
                     ]
+
+            @pl.when(parent > 0)
+            def _():
+                send_out(chunk, parent - 1)
+
             return carry
 
         lax.fori_loop(0, per_device, one_parent, 0)
 
     def disaggregate(chunk, first, last):
         rows = slice(chunk * LANES, (chunk + 1) * LANES)
-        sample = iota((LANES, edge), 1)
+        sample = iota((edge, LANES), 0)
         mats = []
         for shift in (0, gap):
-            high, low = split(stencil(sample - shift, phi_index[rows], phi_weight[rows], 1))
+            high, low = split(stencil(sample - shift, phi_index_t[:, rows], phi_weight_t[:, rows], 0).T)
             mats.append((jnp.concatenate([high, high], axis=0), low))
 
         def one_parent(parent, carry):
+            if last:
+                returned_part(chunk, parent)
             for part in range(parts):
                 for owner in range(samps):
                     grid_sum[part, owner * theta_rows : (owner + 1) * theta_rows] = incoming[chunk][
@@ -290,7 +325,7 @@
                     ]
 
             def one_child(kid, inner):
-                spot = octant[parent * kids + kid]
+                spot = octant[parent, kid]
                 real, imag = grid_sum[0], grid_sum[1]
                 cos_part = cosines[chunk][spot]
                 sin_part = sines[chunk][spot]
@@ -334,14 +369,6 @@
 
         lax.fori_loop(0, per_device, one_parent, 0)
 
-    def send_out(chunk):
-        def one(step, carry):
-            out_copy(chunk, lax.rem(me + step, samps), me).start()
-            return carry
-
-        lax.fori_loop(1, samps, one, 0)
-        keep(chunk).start()
-
     load_child.start()
     for chunk in range(chunks):
         load_angle(chunk).start()
@@ -351,13 +378,12 @@
     load_angle(0).wait()
     turn(0)
     load_child.wait()
+    pl.semaphore_wait(barrier, samps - 1 + len(bits))
     aggregate(0)
     for chunk in range(1, chunks):
         load_angle(chunk).wait()
         turn(chunk)
-        if chunk == 1:
-            pl.semaphore_wait(barrier, samps - 1 + len(bits))
-        send_out(chunk - 1)
+        send_last(chunk - 1)
         aggregate(chunk)
 
     def arrive_and_share(chunk):
@@ -387,16 +413,15 @@
             hop_arrival(chunk, mask).wait_recv()
         load(chunk).wait()
 
-        def receivers(step, carry):
-            peer = lax.rem(me + 1 + step, samps)
-
-            def one(slot, inner):
-                row = (peer * per_device + slot) * partners
+        def receivers(slot, carry):
+            def one(step, inner):
+                peer = lax.rem(me + 1 + step, samps)
+                row = (group * samps + peer) * per_device + slot
                 real = jnp.zeros(results[chunk].shape[3:], jnp.float32)
                 imag = jnp.zeros(results[chunk].shape[3:], jnp.float32)
                 for q in range(partners):
-                    source = src_rows[row + q]
-                    which = disp_rows[row + q]
+                    source = src_rows[q, row]
+                    which = disp_rows[q, row]
                     here = lax.div(source, samps * per_device)
                     rest = lax.rem(source, samps * per_device)
                     from_samp = lax.div(rest, per_device)
@@ -409,18 +434,17 @@
                     imag = imag + (c * b + d * a)
                 results[chunk][peer, slot, 0] = real
                 results[chunk][peer, slot, 1] = imag
+
+                @pl.when(step > 0)
+                def _():
+                    back_part(chunk, slot, lax.rem(me + step, samps), me).start()
+
                 return inner
 
-            lax.fori_loop(0, per_device, one, 0)
-
-            @pl.when(step > 0)
-            def _():
-                peer_before = lax.rem(me + step, samps)
-                back_copy(chunk, peer_before, me).start()
-
-            return carry
-
-        lax.fori_loop(0, samps, receivers, 0)
+            lax.fori_loop(0, samps, one, 0)
+            return carry
+
+        lax.fori_loop(0, per_device, receivers, 0)
 
     def returned(chunk):
         def one(step, carry):
@@ -428,11 +452,20 @@
             back_copy(chunk, there, there).wait_recv()
             return carry
 
+        if chunk < chunks - 1:
+            lax.fori_loop(1, samps, one, 0)
+        back_keep(chunk).wait()
+
+    def returned_part(chunk, parent):
+        def one(step, carry):
+            there = lax.rem(me + samps - step, samps)
+            back_part(chunk, parent, there, there).wait_recv()
+            return carry
+
         lax.fori_loop(1, samps, one, 0)
-        back_keep(chunk).wait()
-
+
+    send_last(chunks - 1)
     arrive_and_share(0)
-    send_out(chunks - 1)
     for chunk in range(chunks):
         if chunk + 1 < chunks:
             arrive_and_share(chunk + 1)
@@ -488,10 +521,6 @@
     half = NT1 // 2
     width = 2 * NP1
     child = child_out.reshape(child_count, parts, half, width)
-    group_rows = parents * samps
-    start = lax.axis_index("box") * group_rows
-    src_rows = lax.dynamic_slice_in_dim(partner_src, start, group_rows, 0).reshape(-1)
-    disp_rows = lax.dynamic_slice_in_dim(partner_disp, start, group_rows, 0).reshape(-1)
     block = (parents, parts, theta_rows, LANES)
     spread = (parents, parts, samps, theta_rows, LANES)
     turns = (octant_count, rows2, LANES)
@@ -506,7 +535,7 @@
     child_in = pl.pallas_call(
         functools.partial(step_kernel, boxes, samps, partners),
         out_shape=jax.ShapeDtypeStruct(child.shape, jnp.float32),
-        in_specs=[scalars] * 3 + [vectors] * 8 + [anywhere] * 3,
+        in_specs=[scalars] * 3 + [vectors] * 4 + [anywhere] * 3,
         out_specs=anywhere,
         scratch_shapes=[
             pltpu.VMEM(child.shape, jnp.float32),
@@ -535,21 +564,17 @@
             dma((chunks, boxes)),
             dma((chunks,)),
             dma((chunks, samps)),
-            dma((chunks, samps)),
+            dma((chunks - 1 + parents, samps)),
         ],
         compiler_params=pltpu.CompilerParams(
             collective_id=0, has_side_effects=True, vmem_limit_bytes=VMEM_LIMIT
         ),
     )(
-        src_rows,
-        disp_rows,
-        child_octant.reshape(-1),
-        theta_index,
-        theta_weight,
+        partner_src.T,
+        partner_disp.T,
+        child_octant,
         theta_index.T,
         theta_weight.T,
-        phi_index,
-        phi_weight,
         phi_index.T,
         phi_weight.T,
         child,

time: 167 us -> 150 us (0.90)
  the two profiles are of different devices: /device:TPU:13 before, /device:TPU:1 now
where the time goes in v3:
time: 150 us
  Pallas kernels  136 us (91%)
  local copies, waits for them, and re-layouts  14.1 us (9%)
    pallas_call x1, Pallas kernels, local(): pl.pallas_call(functools.partial(step_kernel, boxes, samps, partners), ou...  136 us
    reshape x1, local copies, waits for them, and re-layouts, local(): child = child_out.reshape(child_count, parts, half, width)  7.26 us
    reshape x1, local copies, waits for them, and re-layouts, local(): return child_in.reshape(child_count, parts, samples)  6.8 us

profile of v3, /device:TPU:1, one launch (start us, length us, event | category | flops | bytes accessed | tf_op | source)
XLA Modules:
  0.0 150.0 jit_solution(2373312521627297008)
XLA Ops:
  0.0 7.3 %reshape.6.child = f32[32,2,48,384]{3,2,1,0:T(8,128)} reshape(f32[32,2,18432]{2,1,0:T(2,128)} %param.10) | data formatting | bytes 9437184 | tf_op jit(solution)/shard_map/reshape | solution.py:523
  7.3 135.9 %shard_map.100 = f32[32,2,48,384]{3,2,1,0:T(8,128)} custom-call(s32[32,128]{1,0:T(8,128)} %bitcast.8, s32[32,128]{1,0:T(8,128)} %bitcast.9, s32[4,8]{1,0:T(4,128)} %octant.1, s32[4,192]{1,0:T(4,128)} %bitcast.12, f32[4,192]{1,0:T(4,128)} %bitcast.13, s32[4,384]{1,0:T(4,128)} %bitcast.10, f32[4,384]{1,0:T(4,128)} %bitcast.11, ...), custom_call_target="tpu_custom_call" | custom-call | tf_op jit(solution)/shard_map/pallas_call | solution.py:535
  143.2 6.8 %reshape.7 = f32[32,2,18432]{2,1,0:T(2,128)} reshape(f32[32,2,48,384]{3,2,1,0:T(8,128)} %shard_map.100) | data formatting | bytes 9437184 | tf_op jit(solution)/shard_map/reshape | solution.py:584

commit v4 on v3

--- a/solution.py
+++ b/solution.py
@@ -79,7 +79,8 @@
     theta_down,
     *scratch,
 ):
-    count, parts, half, width = child.shape
+    half = NT1 // 2
+    width = 2 * NP1
     chunks = angle.shape[2] // LANES
     rows2 = angle.shape[1]
     sources = scratch[:chunks]
@@ -103,8 +104,9 @@
         back_send,
         back_recv,
     ) = scratch[7 * chunks :]
-    per_device = outgoing[0].shape[0]
-    kids = count // per_device
+    per_device, parts = outgoing[0].shape[:2]
+    kids = child.shape[0] // per_device
+    per_row = width // LANES
     theta_rows = rows2 // samps
     edge = -(-(width // 2) // LANES) * LANES
     gap = edge - width // 2
@@ -223,6 +225,13 @@
         )
 
     load_child = pltpu.make_async_copy(child, field, child_sem)
+
+    def tile(parent, part, place):
+        return (
+            pl.ds(parent * kids, kids),
+            pl.ds(place * parts + part, half, stride=per_row * parts),
+            slice(None),
+        )
 
     def give(parent):
         rows = pl.ds(parent * kids, kids)
@@ -269,7 +278,16 @@
             mats.append(jnp.concatenate([high, low], axis=1))
 
         def one_parent(parent, carry):
-            block = field[pl.ds(parent * kids, kids)].reshape(kids * parts * half, width)
+            block = jnp.concatenate(
+                [
+                    jnp.concatenate(
+                        [field[tile(parent, part, place)].reshape(kids * half, LANES) for place in range(per_row)],
+                        axis=1,
+                    )
+                    for part in range(parts)
+                ],
+                axis=0,
+            )
             pieces = []
             for mat, start in zip(mats, (0, width - edge)):
                 high, low = split(block[:, start : start + edge])
@@ -277,9 +295,9 @@
                 pieces.append(split(both[:, :LANES] + (both[:, LANES:] + dot(low, mat[:, :LANES]))))
             even, odd = pieces
             for slot, piece in enumerate((even[0], odd[0], even[1], odd[1], even[0], odd[0])):
-                piece = piece.reshape(kids, parts, half, LANES)
+                piece = piece.reshape(parts, kids, half, LANES)
                 for part in range(parts):
-                    wide[:, slot * half : (slot + 1) * half, part * LANES : (part + 1) * LANES] = piece[:, part]
+                    wide[:, slot * half : (slot + 1) * half, part * LANES : (part + 1) * LANES] = piece[part]
             grid_sum[...] = jnp.zeros_like(grid_sum)
 
             def one_child(kid, inner):
@@ -354,11 +372,14 @@
                 [left[:, : edge - shared], left[:, edge - shared :] + right[:, :shared], right[:, shared:]],
                 axis=1,
             ).reshape(kids, parts, half, width)
-            spot = pl.ds(parent * kids, kids)
-            if first:
-                field[spot] = joined
-            else:
-                field[spot] += joined
+            for part in range(parts):
+                for place in range(per_row):
+                    spot = tile(parent, part, place)
+                    piece = joined[:, part, :, place * LANES : (place + 1) * LANES]
+                    if first:
+                        field[spot] = piece
+                    else:
+                        field[spot] = field[spot] + piece
             if last:
 
                 @pl.when(parent > 0)
@@ -518,9 +539,9 @@
     partners = partner_src.shape[1]
     theta_rows = rows2 // samps
     chunks = cols2 // LANES
-    half = NT1 // 2
-    width = 2 * NP1
-    child = child_out.reshape(child_count, parts, half, width)
+    tiles = samples // LANES
+    child = child_out.reshape(child_count, parts, tiles, LANES).transpose(0, 2, 1, 3)
+    child = child.reshape(child_count, tiles * parts, LANES)
     block = (parents, parts, theta_rows, LANES)
     spread = (parents, parts, samps, theta_rows, LANES)
     turns = (octant_count, rows2, LANES)
@@ -540,7 +561,7 @@
         scratch_shapes=[
             pltpu.VMEM(child.shape, jnp.float32),
             pltpu.VMEM((kids, 3 * NT1, parts * LANES), jnp.bfloat16),
-            pltpu.VMEM((2, kids * parts, half, 2 * LANES), jnp.bfloat16),
+            pltpu.VMEM((2, kids * parts, NT1 // 2, 2 * LANES), jnp.bfloat16),
             pltpu.VMEM((parts, rows2, LANES), jnp.float32),
             pltpu.VMEM((rows2, 3 * NT1), jnp.bfloat16),
             pltpu.VMEM((2 * NT1, rows2), jnp.bfloat16),
@@ -581,6 +602,7 @@
         shift_angle,
         translation,
     )
+    child_in = child_in.reshape(child_count, tiles, parts, LANES).transpose(0, 2, 1, 3)
     return child_in.reshape(child_count, parts, samples)
 
 

time: 150 us -> 141 us (0.940)
  local copies, waits for them, and re-layouts: 14.1 us -> 4.84 us
    reshape x2 -> x0, local copies, waits for them, and re-layouts: 14.1 us -> none  [the longest x1 7.26 us: local(): child = child_out.reshape(child_count, parts, half, width)]
    unnamed x0 -> x1, local copies, waits for them, and re-layouts: none -> 4.84 us
where the time goes in v4:
time: 141 us
  Pallas kernels  136 us (96%)
  local copies, waits for them, and re-layouts  4.84 us (3%)
    pallas_call x1, Pallas kernels, local(): pl.pallas_call(functools.partial(step_kernel, boxes, samps, partners), ou...  136 us
    unnamed x1, local copies, waits for them, and re-layouts  4.84 us

profile of v4, /device:TPU:1, one launch (start us, length us, event | category | flops | bytes accessed | tf_op | source)
XLA Modules:
  0.0 140.8 jit_solution(14725695471231784147)
XLA Ops:
  0.0 135.9 %shard_map.100 = f32[32,288,128]{2,1,0:T(8,128)} custom-call(s32[32,128]{1,0:T(8,128)} %bitcast.18, s32[32,128]{1,0:T(8,128)} %bitcast.19, s32[4,8]{1,0:T(4,128)} %octant.1, s32[4,192]{1,0:T(4,128)} %bitcast.22, f32[4,192]{1,0:T(4,128)} %bitcast.23, s32[4,384]{1,0:T(4,128)} %bitcast.20, f32[4,384]{1,0:T(4,128)} %bitcast.21, f32[32,288,128]{2,1,0:T(8,128)} %bitcast.17, ...), custom_call_target="tpu_custom_call" | custom-call | tf_op jit(solution)/shard_map/pallas_call | solution.py:556
  135.9 4.8 %copy.14 = f32[32,2,18432]{2,1,0:T(2,128)} copy(f32[32,2,18432]{2,1,0:T(2,128)} %bitcast.16) | data formatting | bytes 9437184
